TPU v7x, 256 devices: a whole 4x4x8 slice. The times are simulated.
256 devices in a mesh: tm: 16 (over y_lo, x, core), col: 16 (over z, y_hi).
Axes of the slice: x: 4, y: 4 (y_hi: 2, y_lo: 2; y = y_hi * 2 + y_lo), z: 8, core: 2. Of those that a mesh axis runs over, the one named last changes fastest.
Arguments:
- panel: bfloat16 [1024, 131072], P('col', 'tm'), may hold values from -60 to 60
- response: float32 [131072], replicated, may hold values from 0.25 to 2.5
Outputs:
- normal: float32 [1024, 1024], P('col', 'tm')
All inputs are finite; a program needn't handle non-finite values.
Results may differ from a plain program's by a relative error of at most 0.0015.
Values may be sent and summed in bfloat16 or wider, within the bound.
No kernel may reach another device: no remote copies, remote signals or barrier semaphores. Data moves between devices by JAX's collectives and lax.ppermute only.
A program may use at most 64 MiB of HBM per device.

v0:
```python
import math
import jax
import jax.numpy as jnp
from jax import lax
from jax.sharding import PartitionSpec as P

EPOCHS = 131072


def angle_tables(row_count, col_count, length):
    row_index = jnp.arange(row_count, dtype=jnp.int32)[:, None]
    col_index = jnp.arange(col_count, dtype=jnp.int32)[None, :]
    phase_index = row_index * col_index % length
    angle = phase_index.astype(jnp.float32) * (2.0 * math.pi / length)
    return (jnp.cos(angle), jnp.sin(angle))


def mixed(form, left, right):
    return jnp.einsum(form, left, right, precision=lax.Precision.HIGHEST)


def split_table(table):
    upper = table.astype(jnp.bfloat16)
    lower = (table - upper.astype(jnp.float32)).astype(jnp.bfloat16)
    return (upper, lower)


def exact_first(table, values):
    upper, lower = split_table(table)
    first = jnp.einsum("kja,jban->kbn", upper, values, preferred_element_type=jnp.float32)
    return first + jnp.einsum("kja,jban->kbn", lower, values, preferred_element_type=jnp.float32)


def whiten_series(series, tables):
    outer_cos, outer_sin, twist_cos, twist_sin, inner_cos, inner_sin, gain_grid = tables
    block_count, item_count, block_len = series.shape
    inner_len = inner_cos.shape[0]
    steps_per_block = block_len // inner_len
    outer_len = block_count * steps_per_block
    values = series.reshape(block_count, item_count, steps_per_block, inner_len)
    fold_cos = outer_cos.reshape(outer_len, block_count, steps_per_block)
    fold_sin = outer_sin.reshape(outer_len, block_count, steps_per_block)
    first_re = exact_first(fold_cos, values)
    first_im = -exact_first(fold_sin, values)
    turn_cos = twist_cos[:, None, :]
    turn_sin = twist_sin[:, None, :]
    turned_re = first_re * turn_cos + first_im * turn_sin
    turned_im = first_im * turn_cos - first_re * turn_sin
    spec_re = mixed("kbn,nl->kbl", turned_re, inner_cos) + mixed(
        "kbn,nl->kbl", turned_im, inner_sin
    )
    spec_im = mixed("kbn,nl->kbl", turned_im, inner_cos) - mixed(
        "kbn,nl->kbl", turned_re, inner_sin
    )
    weight = gain_grid[:, None, :]
    filt_re = spec_re * weight
    filt_im = spec_im * weight
    back_re = mixed("kbl,ln->kbn", filt_re, inner_cos) - mixed("kbl,ln->kbn", filt_im, inner_sin)
    back_im = mixed("kbl,ln->kbn", filt_im, inner_cos) + mixed("kbl,ln->kbn", filt_re, inner_sin)
    untw_re = back_re * turn_cos - back_im * turn_sin
    untw_im = back_im * turn_cos + back_re * turn_sin
    spread_cos = outer_cos.reshape(block_count, steps_per_block, outer_len)
    spread_sin = outer_sin.reshape(block_count, steps_per_block, outer_len)
    result = mixed("jak,kbn->jban", spread_cos, untw_re) - mixed(
        "jak,kbn->jban", spread_sin, untw_im
    )
    result = result * (1.0 / (outer_len * inner_len))
    return result.reshape(block_count, item_count, block_len).astype(jnp.bfloat16)


def on_device(panel, response):
    col_rows, epoch_count = panel.shape
    tm_count = lax.axis_size("tm")
    total_len = tm_count * epoch_count
    inner_len = math.gcd(256, epoch_count)
    outer_len = total_len // inner_len
    outer_cos, outer_sin = angle_tables(outer_len, outer_len, outer_len)
    twist_cos, twist_sin = angle_tables(outer_len, inner_len, total_len)
    inner_cos, inner_sin = angle_tables(inner_len, inner_len, inner_len)
    gain_grid = response.reshape(inner_len, outer_len).T
    tables = (outer_cos, outer_sin, twist_cos, twist_sin, inner_cos, inner_sin, gain_grid)
    grouped = panel.reshape(tm_count, col_rows // tm_count, epoch_count)
    filtered = whiten_series(
        lax.all_to_all(grouped, "tm", split_axis=0, concat_axis=0, tiled=True), tables
    )
    landed = lax.all_to_all(filtered, "tm", split_axis=0, concat_axis=0, tiled=True)
    whitened = landed.reshape(col_rows, epoch_count)
    partial_sum = lax.dot_general(
        whitened,
        lax.all_gather(whitened, "col", axis=0, tiled=True),
        (((1,), (1,)), ((), ())),
        preferred_element_type=jnp.float32,
    )
    summed = lax.psum_scatter(partial_sum, "tm", scatter_dimension=1, tiled=True)
    return summed / EPOCHS


def solution(mesh):
    in_specs = (P("col", "tm"), P())
    out_specs = P("col", "tm")
    return jax.shard_map(
        on_device, mesh=mesh, in_specs=in_specs, out_specs=out_specs, check_vma=False
    )
```

profile of v0, /device:TPU:32, one launch (start us, length us, event | category | flops | bytes accessed | tf_op | source)
XLA Modules:
  0.0 416.5 jit_solution(12158881425810183495)
XLA Ops:
  6.5 0.0 copy-start.2
  6.5 2.3 reshape.89
  8.8 5.4 %all-to-all-start = ((bf16[16,4,8192]{2,1,0:T(4,128)(2,1)}), bf16[16,4,8192]{2,1,0:T(4,128)(2,1)S(1)}, u32[]{:S(2)}, u32[]{:S(2)}) async-start(bf16[16,4,8192]{2,1,0:T(4,128)(2,1)} %reshape.89), calls=%async_computation | async-start | bytes 2097152 | tf_op jit(solution)/shard_map/all_to_all | solution.py:84
  14.2 0.0 all-gather.2.cloned.1.call-start
  14.3 0.0 copy-done.2
  14.3 0.1 reshape.91
  14.4 0.2 copy.8
  14.6 2.1 fusion.79
  16.7 14.0 %all-to-all-done = bf16[16,4,8192]{2,1,0:T(4,128)(2,1)S(1)} async-done(((bf16[16,4,8192]{2,1,0:T(4,128)(2,1)}), bf16[16,4,8192]{2,1,0:T(4,128)(2,1)S(1)}, u32[]{:S(2)}, u32[]{:S(2)}) %all-to-all-start) | async-done | bytes 1048608 | tf_op jit(solution)/shard_map/all_to_all | solution.py:84
  30.7 2.0 reshape.107
  32.7 0.0 copy-start.1
  32.7 5.7 %fusion.43 = f32[512,4,256,1]{2,0,1,3:T(8,128)S(1)} fusion(bf16[16,4,32,256]{3,2,1,0:T(8,128)(2,1)} %reshape.107, s32[16,32]{1,0:T(8,128)S(1)} %multiply_add_fusion.3), kind=kOutput, calls=%fused_computation.58 | convolution fusion | flops 540803072 | bytes 3147776 | tf_op jit(solution)/shard_map/kja,jban->kbn/dot_general | solution.py:30
  38.4 0.0 copy-done.1
  38.4 4.4 %fusion.45 = f32[512,4,256,1]{2,0,1,3:T(8,128)S(1)} fusion(bf16[16,4,32,256]{3,2,1,0:T(8,128)(2,1)S(1)} %copy-done.1, s32[16,32]{1,0:T(8,128)S(1)} %multiply_add_fusion.3), kind=kOutput, calls=%fused_computation.60 | convolution fusion | flops 540803072 | bytes 3147776 | tf_op jit(solution)/shard_map/kja,jban->kbn/dot_general | solution.py:30
  42.8 4.6 %fusion = f32[512,4,256]{2,0,1:T(8,128)S(1)} fusion(f32[512,4,256,1]{2,0,1,3:T(8,128)S(1)} %fusion.43, bf16[16,4,32,256]{3,2,1,0:T(8,128)(2,1)S(1)} %copy-done.1, s32[16,32]{1,0:T(8,128)S(1)} %multiply_add_fusion.3), kind=kOutput, calls=%fused_computation.1 | convolution fusion | flops 542638080 | bytes 5244928 | tf_op jit(solution)/shard_map/kja,jban->kbn/dot_general | solution.py:31
  47.4 4.4 %bitcast_add_fusion.1 = f32[512,4,256]{2,0,1:T(8,128)S(1)} fusion(f32[512,4,256,1]{2,0,1,3:T(8,128)S(1)} %fusion.45, bf16[16,4,32,256]{3,2,1,0:T(8,128)(2,1)S(1)} %copy-done.1, s32[16,32]{1,0:T(8,128)S(1)} %multiply_add_fusion.3), kind=kOutput, calls=%fused_computation.2 | convolution fusion | flops 542113792 | bytes 5244928 | tf_op jit(solution)/shard_map/kja,jban->kbn/dot_general | solution.py:31
  51.9 3.1 fusion.71
  54.9 3.1 fusion.75
  58.0 3.4 subtract_multiply_fusion
  61.4 2.8 fusion.69
  64.3 3.2 add_multiply_fusion
  67.4 2.8 fusion.73
  70.3 3.3 convolution_add_fusion
  73.6 2.9 convolution_subtract_fusion
  76.6 7.8 %fusion.1 = f32[4,256,16,32]{1,3,2,0:T(8,128)S(1)} fusion(f32[512,4,256]{2,0,1:T(8,128)S(1)} %convolution_subtract_fusion, f32[512,4,256]{2,0,1:T(8,128)S(1)} %convolution_add_fusion, f32[512,256]{1,0:T(8,128)S(1)} %get-tuple-element.5, f32[512,256]{1,0:T(8,128)S(1)} %get-tuple-element.6, s32[16,32]{1,0:T(8,128)S(1)} %multiply_add_fusion.3), kind=kOutput, calls=%fused_computation.3 | convolution fusion | flops 3226468352 | bytes 7342080 | tf_op jit(solution)/shard_map/jak,kbn->jban/dot_general | solution.py:19
  84.4 7.7 %fusion.13 = bf16[16,4,32,256]{3,2,0,1:T(8,128)(2,1)S(1)} fusion(f32[4,256,16,32]{1,3,2,0:T(8,128)S(1)} %fusion.1, f32[512,4,256]{2,0,1:T(8,128)S(1)} %convolution_add_fusion, f32[512,4,256]{2,0,1:T(8,128)S(1)} %convolution_subtract_fusion, f32[512,256]{1,0:T(8,128)S(1)} %get-tuple-element.5, f32[512,256]{1,0:T(8,128)S(1)} %get-tuple-element.6, ...), kind=kOutput, calls=%fused_computation.26 | convolution fusion | flops 3228041216 | bytes 8390656 | tf_op jit(solution)/shard_map/jak,kbn->jban/dot_general | solution.py:19
  92.1 0.5 convert_element_type.101
  92.7 0.8 copy.9
  93.5 19.1 %all_to_all.10 = bf16[16,4,8192]{2,1,0:T(4,128)(2,1)S(1)} all-to-all(bf16[16,4,8192]{2,1,0:T(4,128)(2,1)S(1)} %copy.9), channel_id=1, replica_groups=mesh['tm'=16,'col'=16] {'tm'}, dimensions={0} | all-to-all | bytes 2097152 | tf_op jit(solution)/shard_map/all_to_all | solution.py:86
  112.6 1.1 reshape.92
  113.6 0.0 copy-start
  113.6 0.0 all-gather.2.cloned.1.call-update
  113.7 0.0 reduce-scatter.4.cloned.1.call-start
  113.7 222.7 %all-gather.2.cloned.1.call-done = bf16[1024,8192]{1,0:T(8,128)(2,1)} async-done(((bf16[64,8192]{1,0:T(8,128)(2,1)}), bf16[1024,8192]{1,0:T(8,128)(2,1)}) %all-gather.2.cloned.1.call-update) | async-done | bytes 16777232 | tf_op jit(solution)/shard_map/all_gather | solution.py:90
  336.5 0.0 copy-done
  336.5 8.9 %convolution_bitcast_fusion = f32[1024,64]{1,0:T(8,128)} fusion(bf16[64,8192]{1,0:T(8,128)(2,1)S(1)} %copy-done, bf16[1024,8192]{1,0:T(8,128)(2,1)} %all-gather.2.cloned.1.call-done), kind=kOutput, calls=%fused_computation.27 | convolution fusion | flops 1073741824 | bytes 18087936
  345.4 0.0 reduce-scatter.4.cloned.1.call-update
  345.4 62.6 %reduce-scatter.4.cloned.1.call-done = f32[64,64]{1,0:T(8,128)} async-done(((f32[1024,64]{1,0:T(8,128)}), f32[64,64]{1,0:T(8,128)}) %reduce-scatter.4.cloned.1.call-update) | async-done | bytes 16400
  408.0 0.8 copy.18
  408.9 0.6 broadcast_multiply_fusion
  (1 shorter events, 0.0 us)
Async XLA Ops:
  6.5 7.8 %copy-start.2 = (f32[131072]{0:T(1024)S(1)}, f32[131072]{0:T(1024)}, u32[]{:S(2)}) copy-start(f32[131072]{0:T(1024)} %param.3) | copy-start | bytes 1572868
  8.8 21.9 %all-to-all-start = ((bf16[16,4,8192]{2,1,0:T(4,128)(2,1)}), bf16[16,4,8192]{2,1,0:T(4,128)(2,1)S(1)}, u32[]{:S(2)}, u32[]{:S(2)}) async-start(bf16[16,4,8192]{2,1,0:T(4,128)(2,1)} %reshape.89), calls=%async_computation | async-start | bytes 2097152 | tf_op jit(solution)/shard_map/all_to_all | solution.py:84
  14.2 322.2 %all-gather.2.cloned.1.call-start = ((), (), s32[]{:S(2)}) async-start(), calls=%async_computation.3 | async-start | bytes 17825792 | tf_op jit(solution)/shard_map/all_gather | solution.py:90
  32.7 5.7 %copy-start.1 = (bf16[16,4,32,256]{3,2,1,0:T(8,128)(2,1)S(1)}, bf16[16,4,32,256]{3,2,1,0:T(8,128)(2,1)}, u32[]{:S(2)}) copy-start(bf16[16,4,32,256]{3,2,1,0:T(8,128)(2,1)} %reshape.107) | copy-start | bytes 3145732
  113.6 222.8 %copy-start = (bf16[64,8192]{1,0:T(8,128)(2,1)S(1)}, bf16[64,8192]{1,0:T(8,128)(2,1)}, u32[]{:S(2)}) copy-start(bf16[64,8192]{1,0:T(8,128)(2,1)} %reshape.92) | copy-start | bytes 3145732
  113.7 294.4 %reduce-scatter.4.cloned.1.call-start = ((), (), s32[]{:S(2)}) async-start(), calls=%async_computation.4 | async-start | bytes 557056
Sparse Core Ops, SparseCore 0:
  113.8 222.6 all-gather.1
  345.5 62.4 reduce-scatter.3
where the time goes:
time: 420 us; the launch traced here: 417 us
  waiting for transfers between devices  299 us (71%)
  matrix products  68.2 us (16%)
  blocking collectives  19.1 us (5%)
  between operations  13.8 us (3%)
  local copies, waits for them, and re-layouts  7.8 us (2%)
  starting transfers between devices  5.5 us (1%)
    all_gather x1, waiting for transfers between devices, on_device(): lax.all_gather(whitened, 'col', axis=0, tiled=True)  223 us
    unnamed x3, waiting for transfers between devices  62.7 us
    dot_general x10, matrix products, mixed(): return jnp.einsum(form, left, right, precision=lax.Precision.HIGHEST)  40.2 us
    all_to_all x1, blocking collectives, on_device(): lax.all_to_all(filtered, 'tm', split_axis=0, concat_axis=0, tiled=True)  19.1 us
    all_to_all x1, waiting for transfers between devices, on_device(): lax.all_to_all(grouped, 'tm', split_axis=0, concat_axis=0, tiled=True)  14 us
    dot_general x2, matrix products, exact_first(): jnp.einsum('kja,jban->kbn', upper, values, preferred_element_type=jnp.flo...  10.1 us
    dot_general x2, matrix products, exact_first(): jnp.einsum('kja,jban->kbn', lower, values, preferred_element_type=jnp.flo...  9.04 us
    unnamed x1, matrix products  8.9 us
  transfers between devices with their start and end apart: 3, of which 3 were waited for; matrix products, arithmetic and copies ran while one was open for 1% of the time, Pallas kernels for 0%

commit v1 on v0

--- a/solution.py
+++ b/solution.py
@@ -5,6 +5,16 @@
 from jax.sharding import PartitionSpec as P
 
 EPOCHS = 131072
+
+
+def edge_name(shard_axis, work_x):
+    row_out = jnp.concatenate(
+        lax.all_to_all(
+            jnp.stack(tuple((work_x for _ in range(lax.axis_size(shard_axis))))), shard_axis, 0, 0
+        ),
+        axis=0,
+    )
+    return row_out
 
 
 def angle_tables(row_count, col_count, length):
@@ -87,7 +97,7 @@
     whitened = landed.reshape(col_rows, epoch_count)
     partial_sum = lax.dot_general(
         whitened,
-        lax.all_gather(whitened, "col", axis=0, tiled=True),
+        edge_name("col", whitened),
         (((1,), (1,)), ((), ())),
         preferred_element_type=jnp.float32,
     )

time: 420 us -> 566 us (1.35)
  blocking collectives: 19.1 us -> 395 us
  waiting for transfers between devices: 299 us -> 72.7 us
    all_to_all x0 -> x1, blocking collectives: none -> 376 us  [edge_name(): lax.all_to_all(jnp.stack(tuple((work_x for _ in range(lax.axis_size(shard...]
    all_gather x1 -> x0, waiting for transfers between devices: 223 us -> none  [on_device(): lax.all_gather(whitened, 'col', axis=0, tiled=True)]
    unnamed x3 -> x2, waiting for transfers between devices: 62.7 us -> 58.7 us
  transfers between devices with their start and end apart: 3 -> 2, of which waited for: 3 -> 2; matrix products, arithmetic and copies ran while one was open for 1% -> 0% of each run, Pallas kernels for 0% -> 0%
where the time goes in v1:
time: 566 us; the launch traced here: 563 us
  blocking collectives  395 us (70%)
  waiting for transfers between devices  72.7 us (13%)
  matrix products  64.9 us (11%)
  between operations  13.8 us (2%)
  local copies, waits for them, and re-layouts  8.52 us (2%)
    all_to_all x1, blocking collectives, edge_name(): lax.all_to_all(jnp.stack(tuple((work_x for _ in range(lax.axis_size(shard...  376 us
    unnamed x2, waiting for transfers between devices  58.7 us
    dot_general x10, matrix products, mixed(): return jnp.einsum(form, left, right, precision=lax.Precision.HIGHEST)  40.1 us
    all_to_all x1, blocking collectives, on_device(): lax.all_to_all(filtered, 'tm', split_axis=0, concat_axis=0, tiled=True)  19.1 us
    all_to_all x1, waiting for transfers between devices, on_device(): lax.all_to_all(grouped, 'tm', split_axis=0, concat_axis=0, tiled=True)  14 us
  transfers between devices with their start and end apart: 2, of which 2 were waited for; matrix products, arithmetic and copies ran while one was open for 0% of the time, Pallas kernels for 0%

profile of v1, /device:TPU:32, one launch (start us, length us, event | category | flops | bytes accessed | tf_op | source)
XLA Modules:
  0.0 562.9 jit_solution(6022214569599451113)
XLA Ops:
  6.5 0.0 copy-start.1
  6.5 2.3 reshape.94
  8.8 5.4 all-to-all-start
  14.3 0.0 reduce-scatter.4.cloned.1.call-start
  14.3 0.0 copy-done.1
  14.3 0.1 reshape.96
  14.4 0.2 copy.8
  14.6 2.1 fusion.79
  16.7 14.0 %all-to-all-done = bf16[16,4,8192]{2,1,0:T(4,128)(2,1)S(1)} async-done(((bf16[16,4,8192]{2,1,0:T(4,128)(2,1)}), bf16[16,4,8192]{2,1,0:T(4,128)(2,1)S(1)}, u32[]{:S(2)}, u32[]{:S(2)}) %all-to-all-start) | async-done | bytes 1048608 | tf_op jit(solution)/shard_map/all_to_all | solution.py:94
  30.7 1.8 reshape.113
  32.5 0.0 copy-start
  32.5 5.7 %fusion.43 = f32[512,4,256,1]{2,0,1,3:T(8,128)S(1)} fusion(bf16[16,4,32,256]{3,2,1,0:T(8,128)(2,1)} %reshape.113, s32[16,32]{1,0:T(8,128)S(1)} %multiply_add_fusion.3), kind=kOutput, calls=%fused_computation.58 | convolution fusion | flops 540803072 | bytes 3147776 | tf_op jit(solution)/shard_map/kja,jban->kbn/dot_general | solution.py:40
  38.2 0.0 copy-done
  38.3 4.4 fusion.45
  42.7 5.0 fusion
  47.6 4.4 bitcast_add_fusion.1
  52.1 3.1 fusion.71
  55.1 3.1 fusion.75
  58.2 3.3 subtract_multiply_fusion
  61.6 2.8 fusion.69
  64.4 3.2 add_multiply_fusion
  67.6 2.8 fusion.73
  70.4 3.1 convolution_add_fusion
  73.5 2.9 convolution_subtract_fusion
  76.5 8.0 %fusion.1 = f32[4,256,16,32]{1,3,2,0:T(8,128)S(1)} fusion(f32[512,4,256]{2,0,1:T(8,128)S(1)} %convolution_subtract_fusion, f32[512,4,256]{2,0,1:T(8,128)S(1)} %convolution_add_fusion, f32[512,256]{1,0:T(8,128)S(1)} %get-tuple-element.5, f32[512,256]{1,0:T(8,128)S(1)} %get-tuple-element.6, s32[16,32]{1,0:T(8,128)S(1)} %multiply_add_fusion.3), kind=kOutput, calls=%fused_computation.3 | convolution fusion | flops 3226468352 | bytes 7342080 | tf_op jit(solution)/shard_map/jak,kbn->jban/dot_general | solution.py:29
  84.5 7.7 %fusion.13 = bf16[16,4,32,256]{3,2,0,1:T(8,128)(2,1)S(1)} fusion(f32[4,256,16,32]{1,3,2,0:T(8,128)S(1)} %fusion.1, f32[512,4,256]{2,0,1:T(8,128)S(1)} %convolution_add_fusion, f32[512,4,256]{2,0,1:T(8,128)S(1)} %convolution_subtract_fusion, f32[512,256]{1,0:T(8,128)S(1)} %get-tuple-element.5, f32[512,256]{1,0:T(8,128)S(1)} %get-tuple-element.6, ...), kind=kOutput, calls=%fused_computation.26 | convolution fusion | flops 3228041216 | bytes 8390656 | tf_op jit(solution)/shard_map/jak,kbn->jban/dot_general | solution.py:29
  92.2 0.5 convert_element_type.101
  92.8 0.8 copy.9
  93.6 19.1 %all_to_all.15 = bf16[16,4,8192]{2,1,0:T(4,128)(2,1)S(1)} all-to-all(bf16[16,4,8192]{2,1,0:T(4,128)(2,1)S(1)} %copy.9), channel_id=1, replica_groups=mesh['tm'=16,'col'=16] {'tm'}, dimensions={0} | all-to-all | bytes 2097152 | tf_op jit(solution)/shard_map/all_to_all | solution.py:96
  112.7 0.3 reshape.97
  112.9 1.7 stack.3
  114.7 375.8 %all_to_all.16 = bf16[16,64,8192]{2,1,0:T(8,128)(2,1)S(1)} all-to-all(bf16[16,64,8192]{2,1,0:T(8,128)(2,1)S(1)} %stack.3), channel_id=1, replica_groups=mesh['tm'=16,'col'=16] {'col'}, dimensions={0} | all-to-all | bytes 33554432 | tf_op jit(solution)/shard_map/all_to_all | solution.py:12
  490.5 5.3 convolution_bitcast_fusion
  495.8 0.0 reduce-scatter.4.cloned.1.call-update
  495.8 58.7 %reduce-scatter.4.cloned.1.call-done = f32[64,64]{1,0:T(8,128)} async-done(((f32[1024,64]{1,0:T(8,128)}), f32[64,64]{1,0:T(8,128)}) %reduce-scatter.4.cloned.1.call-update) | async-done | bytes 16400
  554.4 0.8 copy.18
  555.3 0.6 broadcast_multiply_fusion
  (1 shorter events, 0.0 us)
Async XLA Ops:
  6.5 7.8 %copy-start.1 = (f32[131072]{0:T(1024)S(1)}, f32[131072]{0:T(1024)}, u32[]{:S(2)}) copy-start(f32[131072]{0:T(1024)} %param.3) | copy-start | bytes 1572868
  8.8 21.9 %all-to-all-start = ((bf16[16,4,8192]{2,1,0:T(4,128)(2,1)}), bf16[16,4,8192]{2,1,0:T(4,128)(2,1)S(1)}, u32[]{:S(2)}, u32[]{:S(2)}) async-start(bf16[16,4,8192]{2,1,0:T(4,128)(2,1)} %reshape.94), calls=%async_computation | async-start | bytes 2097152 | tf_op jit(solution)/shard_map/all_to_all | solution.py:94
  14.3 540.2 %reduce-scatter.4.cloned.1.call-start = ((), (), s32[]{:S(2)}) async-start(), calls=%async_computation.4 | async-start | bytes 557056
  32.5 5.7 %copy-start = (bf16[16,4,32,256]{3,2,1,0:T(8,128)(2,1)S(1)}, bf16[16,4,32,256]{3,2,1,0:T(8,128)(2,1)}, u32[]{:S(2)}) copy-start(bf16[16,4,32,256]{3,2,1,0:T(8,128)(2,1)} %reshape.113) | copy-start | bytes 3145732
Sparse Core Ops, SparseCore 0:
  495.9 58.4 reduce-scatter.3
